TPU v7x, 128 devices: a whole 4x4x4 slice. The times are simulated.
128 devices in a mesh: dp: 8 (over z, y_lo), cp: 16 (over x, y_hi, core).
Axes of the slice: x: 4, y: 4 (y_hi: 2, y_lo: 2; y = y_hi * 2 + y_lo), z: 4, core: 2. Of those that a mesh axis runs over, the one named last changes fastest.
Arguments:
- table_rows: bfloat16 [262144, 1024], P(('dp', 'cp')), may hold values from -6 to 6
- row_scales: float32 [262144], P(('dp', 'cp')), may hold values from 0.25 to 4
- owners: int32 [16384, 1], P(('dp', 'cp')), may hold values from 0 to 127; in each aligned block of 128 rows (0 to 127, 128 to 255, ...) at most 2 rows name the same one
- shard_rows: int32 [16384], P(('dp', 'cp')), may hold values from 0 to 2047
- history_lengths: int32 [8, 3], P('dp'), may hold values from 1 to 1024, 2048 in all within a row
- input_weight: bfloat16 [1024, 4096], replicated, may hold values from -0.1875 to 0.1875
- output_weight: bfloat16 [1024, 1024], replicated, may hold values from -0.1875 to 0.1875
- cotangent: bfloat16 [16384, 1024], P(('dp', 'cp')), may hold values from -6 to 6
Outputs:
- layer_out: bfloat16 [16384, 1024], P(('dp', 'cp'))
- table_grad: float32 [262144, 1024], P(('dp', 'cp'))
Inputs may be any that keep to these rules, and one draw needn't show every extreme that they name: `owners`: among the events of one device no shard is named more than 2 times, and some device names one shard exactly 2 times. `history_lengths`: the 3 lengths of a cycle group sum to 2048; the longest is exactly 1024.
All inputs are finite; a program needn't handle non-finite values.
Results may differ from a plain program's by a relative error of at most 0.0043.
Values may be sent and summed in bfloat16 or wider, within the bound.
No kernel may reach another device: no remote copies, remote signals or barrier semaphores. Data moves between devices by JAX's collectives and lax.ppermute only.
A program may use at most 128 MiB of HBM per device.

v0:
```python
import jax
import jax.numpy as jnp
from jax import lax
from jax.sharding import PartitionSpec as P

HEADS = 8
EPSILON = 1e-05


def doc_bounds(lengths, positions):
    ends_at = jnp.cumsum(lengths)
    begins_at = ends_at - lengths
    inside = (positions[:, None] >= begins_at[None, :]) & (positions[:, None] < ends_at[None, :])
    doc_first = jnp.sum(jnp.where(inside, begins_at[None, :], 0), axis=1)
    doc_length = jnp.sum(jnp.where(inside, lengths[None, :], 0), axis=1).astype(jnp.float32)
    return (doc_first, doc_length)


def normalize(values):
    center = jnp.mean(values, axis=-1, keepdims=True)
    shifted = values - center
    inv_spread = lax.rsqrt(jnp.mean(shifted * shifted, axis=-1, keepdims=True) + EPSILON)
    return (shifted * inv_spread, inv_spread)


def normalize_back(grad_in, normed, inv_spread):
    return inv_spread * (
        grad_in
        - jnp.mean(grad_in, axis=-1, keepdims=True)
        - normed * jnp.mean(grad_in * normed, axis=-1, keepdims=True)
    )


def score_block(queries, key_block, query_pos, query_first, key_pos):
    scaling = queries.shape[-1] ** (-0.5)
    scores = (
        jnp.einsum("qhe,khe->hqk", queries, key_block, preferred_element_type=jnp.float32) * scaling
    )
    allowed = (key_pos[None, :] >= query_first[:, None]) & (key_pos[None, :] <= query_pos[:, None])
    return (scores, allowed[None])


def forward_part(queries, key_block, value_block, query_pos, query_first, query_length, key_pos):
    scores, allowed = score_block(queries, key_block, query_pos, query_first, key_pos)
    weights = jnp.where(
        allowed, scores * jax.nn.sigmoid(scores) / query_length[None, :, None], 0.0
    ).astype(jnp.bfloat16)
    return jnp.einsum("hqk,khe->qhe", weights, value_block, preferred_element_type=jnp.float32)


def backward_part(
    queries, key_block, value_block, grad_out, query_pos, query_first, query_length, key_pos
):
    scores, allowed = score_block(queries, key_block, query_pos, query_first, key_pos)
    sigmoid_part = jax.nn.sigmoid(scores)
    weights = jnp.where(allowed, scores * sigmoid_part / query_length[None, :, None], 0.0).astype(
        jnp.bfloat16
    )
    grad_weights = jnp.einsum(
        "qhe,khe->hqk", grad_out, value_block, preferred_element_type=jnp.float32
    )
    silu_slope = sigmoid_part * (1.0 + scores * (1.0 - sigmoid_part))
    scaling = queries.shape[-1] ** (-0.5)
    grad_scores = jnp.where(
        allowed, grad_weights * silu_slope / query_length[None, :, None] * scaling, 0.0
    ).astype(jnp.bfloat16)
    grad_query = jnp.einsum(
        "hqk,khe->qhe", grad_scores, key_block, preferred_element_type=jnp.float32
    )
    grad_key = jnp.einsum("hqk,qhe->khe", grad_scores, queries, preferred_element_type=jnp.float32)
    grad_value = jnp.einsum("hqk,qhe->khe", weights, grad_out, preferred_element_type=jnp.float32)
    return (grad_query, grad_key, grad_value)


def sweep(kernel, running, key_total, block_size, lowest, highest):

    def advance(block_index, current):
        block_start = block_index * block_size
        needed = (block_start <= highest) & (block_start + block_size > lowest)
        return lax.cond(
            needed,
            lambda state: kernel(state, block_start, block_size),
            lambda state: state,
            current,
        )

    return lax.fori_loop(0, key_total // block_size, advance, running)


def per_device(
    table_rows,
    row_scales,
    owners,
    shard_rows,
    history_lengths,
    input_weight,
    output_weight,
    cotangent,
):
    row_count = owners.shape[0]
    model_width = table_rows.shape[1]
    head_count = HEADS
    head_size = model_width // head_count
    devices = lax.axis_size(("dp", "cp"))
    capacity = max(2, 2 * row_count // devices)
    target = owners[:, 0]
    matches = (target[:, None] == jnp.arange(devices, dtype=jnp.int32)[None, :]).astype(jnp.int32)
    before = jnp.cumsum(matches, axis=0) - matches
    ranked = jnp.sum(before * matches, axis=1)
    placed = target * capacity + ranked
    requests = jnp.zeros((devices * capacity,), jnp.int32).at[placed].set(shard_rows + 1)
    incoming = lax.all_to_all(
        requests.reshape(devices, capacity), ("dp", "cp"), split_axis=0, concat_axis=0, tiled=True
    ).reshape(-1)
    wanted = incoming > 0
    lookup = jnp.maximum(incoming - 1, 0)
    fetched = jnp.where(
        wanted[:, None], table_rows[lookup].astype(jnp.float32) * row_scales[lookup][:, None], 0.0
    )
    returned = lax.all_to_all(
        fetched.reshape(devices, capacity, model_width),
        ("dp", "cp"),
        split_axis=0,
        concat_axis=0,
        tiled=True,
    )
    embedded = returned.reshape(devices * capacity, model_width)[placed]
    normed, inv_embed = normalize(embedded)
    projected = jnp.dot(
        normed.astype(jnp.bfloat16), input_weight, preferred_element_type=jnp.float32
    )
    activated = (projected * jax.nn.sigmoid(projected)).astype(jnp.bfloat16)
    gate_rows = activated[:, :model_width]
    value_rows = activated[:, model_width : 2 * model_width]
    query_rows = activated[:, 2 * model_width : 3 * model_width]
    key_rows = activated[:, 3 * model_width :]
    lengths = history_lengths[0]
    cycle_pos = lax.axis_index("cp") * row_count + jnp.arange(row_count, dtype=jnp.int32)
    query_first, query_length = doc_bounds(lengths, cycle_pos)
    lowest = jnp.min(query_first)
    highest = cycle_pos[row_count - 1]
    key_all, value_all = (
        lax.all_gather(key_rows, "cp", axis=0, tiled=True),
        lax.all_gather(value_rows, "cp", axis=0, tiled=True),
    )
    key_total = key_all.shape[0]
    queries = query_rows.reshape(row_count, head_count, head_size)

    def key_slices(block_start, piece_size):
        key_block = key_all.reshape(piece_size, head_count, head_size)
        value_block = value_all.reshape(piece_size, head_count, head_size)
        key_pos = block_start + jnp.arange(piece_size, dtype=jnp.int32)
        return (key_block, value_block, key_pos)

    def forward_kernel(running, block_start, piece_size):
        key_block, value_block, key_pos = key_slices(block_start, piece_size)
        return running + forward_part(
            queries, key_block, value_block, cycle_pos, query_first, query_length, key_pos
        )

    zeros_local = jnp.zeros((row_count, head_count, head_size), jnp.float32)
    attention = sweep(forward_kernel, zeros_local, key_total, key_total, lowest, highest).reshape(
        row_count, model_width
    )
    attn_norm, inv_attn = normalize(attention)
    mixed = attn_norm * gate_rows.astype(jnp.float32)
    output = embedded + jnp.dot(
        mixed.astype(jnp.bfloat16), output_weight, preferred_element_type=jnp.float32
    )
    layer_out = output.astype(jnp.bfloat16)
    grad_mixed = jnp.einsum(
        "rk,dk->rd", cotangent, output_weight, preferred_element_type=jnp.float32
    )
    grad_gate = grad_mixed * attn_norm
    grad_attn = normalize_back(
        grad_mixed * gate_rows.astype(jnp.float32), attn_norm, inv_attn
    ).astype(jnp.bfloat16)
    grad_heads = grad_attn.reshape(row_count, head_count, head_size)
    zeros_all = jnp.zeros((key_total, head_count, head_size), jnp.float32)

    def backward_kernel(running, block_start, piece_size):
        key_block, value_block, key_pos = key_slices(block_start, piece_size)
        grad_query, grad_key, grad_value = backward_part(
            queries,
            key_block,
            value_block,
            grad_heads,
            cycle_pos,
            query_first,
            query_length,
            key_pos,
        )
        return (running[0] + grad_query, grad_key, grad_value)

    grad_query, grad_key_all, grad_value_all = sweep(
        backward_kernel, (zeros_local, zeros_all, zeros_all), key_total, key_total, lowest, highest
    )
    grad_key, grad_value = (
        lax.psum_scatter(
            grad_key_all.reshape(key_total, model_width), "cp", scatter_dimension=0, tiled=True
        ),
        lax.psum_scatter(
            grad_value_all.reshape(key_total, model_width), "cp", scatter_dimension=0, tiled=True
        ),
    )
    grad_act = jnp.concatenate(
        [grad_gate, grad_value, grad_query.reshape(row_count, model_width), grad_key], axis=1
    )
    sigmoid_part = jax.nn.sigmoid(projected)
    grad_proj = (grad_act * sigmoid_part * (1.0 + projected * (1.0 - sigmoid_part))).astype(
        jnp.bfloat16
    )
    grad_norm = jnp.einsum("rk,dk->rd", grad_proj, input_weight, preferred_element_type=jnp.float32)
    grad_embed = cotangent.astype(jnp.float32) + normalize_back(grad_norm, normed, inv_embed)
    outgoing = jnp.zeros((devices * capacity, model_width), jnp.float32).at[placed].set(grad_embed)
    arrived = lax.all_to_all(
        outgoing.reshape(devices, capacity, model_width),
        ("dp", "cp"),
        split_axis=0,
        concat_axis=0,
        tiled=True,
    ).reshape(devices * capacity, model_width)
    summed = (
        jnp.zeros(table_rows.shape, jnp.float32)
        .at[lookup]
        .add(jnp.where(wanted[:, None], arrived, 0.0))
    )
    table_grad = summed * row_scales[:, None]
    return (layer_out, table_grad)


def solution(mesh):
    return jax.shard_map(
        per_device,
        mesh=mesh,
        in_specs=(
            P(("dp", "cp"), None),
            P(("dp", "cp")),
            P(("dp", "cp"), None),
            P(("dp", "cp")),
            P("dp", None),
            P(),
            P(),
            P(("dp", "cp"), None),
        ),
        out_specs=(P(("dp", "cp"), None), P(("dp", "cp"), None)),
        check_vma=False,
    )
```

profile of v0, /device:TPU:1, one launch (start us, length us, event | category | flops | bytes accessed | tf_op | source)
XLA Modules:
  0.0 501.4 jit_solution(9689500098973985464)
XLA Ops:
  11.5 20.8 %all_to_all.19 = s32[128,1,2]{2,1,0:T(1,128)S(1)} all-to-all(s32[128,1,2]{2,1,0:T(1,128)S(1)} %bitcast.137), channel_id=1, replica_groups=mesh['dp'=8,'cp'=16] {'dp','cp'}, dimensions={0} | all-to-all | bytes 2048 | tf_op jit(solution)/shard_map/all_to_all | solution.py:112
  33.2 1.9 gather_fusion.1
  35.3 5.1 %gather_fusion = bf16[256,1024]{1,0:T(8,128)(2,1)} fusion(bf16[2048,1024]{1,0:T(8,128)(2,1)} %param.12, s32[1024]{0:T(1024)S(1)} %pad_clamp_fusion.1), kind=kCustom, calls=%fused_computation | custom fusion | bytes 1049600 | tf_op jit(solution)/shard_map/gather | solution.py:118
  43.6 5.6 %all-to-all-start.1 = ((f32[128,2,1024]{2,1,0:T(2,128)}), f32[128,2,1024]{2,1,0:T(2,128)}, u32[]{:S(2)}, u32[]{:S(2)}) async-start(f32[128,2,1024]{2,1,0:T(2,128)} %multiply_select_fusion), calls=%async_computation.1 | async-start | bytes 2097152 | tf_op jit(solution)/shard_map/all_to_all | solution.py:120
  49.2 18.6 %all-to-all-done.1 = f32[128,2,1024]{2,1,0:T(2,128)} async-done(((f32[128,2,1024]{2,1,0:T(2,128)}), f32[128,2,1024]{2,1,0:T(2,128)}, u32[]{:S(2)}, u32[]{:S(2)}) %all-to-all-start.1) | async-done | bytes 1048608 | tf_op jit(solution)/shard_map/all_to_all | solution.py:120
  67.9 1.9 reshape.277
  73.8 6.3 %multiply_convert_fusion = (bf16[128,4096]{1,0:T(8,128)(2,1)S(1)}, f32[128,4096]{1,0:T(8,128)}) fusion(bf16[1024,4096]{1,0:T(8,128)(2,1)} %param.17, f32[128,1024]{1,0:T(8,128)} %gather_fusion.2, f32[128]{0:T(128)S(1)} %add_rsqrt_fusion.1, f32[128]{0:T(128)S(1)} %broadcast_multiply_fusion.6), kind=kOutput, calls=%fused_computation.60 | convolution fusion | flops 1076756480 | bytes 12059648 | tf_op jit(solution)/shard_map/dot_general | solution.py:129
  85.7 49.2 %all-gather.5.cloned.1.call-done = bf16[2048,1024]{1,0:T(8,128)(2,1)} async-done(((bf16[128,1024]{1,0:T(8,128)(2,1)}), bf16[2048,1024]{1,0:T(8,128)(2,1)}) %all-gather.5.cloned.1.call-update) | async-done | bytes 4194320 | tf_op jit(solution)/shard_map/all_gather | solution.py:144
  134.9 57.9 %all-gather.3.cloned.1.call-done = bf16[2048,1024]{1,0:T(8,128)(2,1)} async-done(((bf16[128,1024]{1,0:T(8,128)(2,1)}), bf16[2048,1024]{1,0:T(8,128)(2,1)}) %all-gather.3.cloned.1.call-update) | async-done | bytes 4194320 | tf_op jit(solution)/shard_map/all_gather | solution.py:143
  192.9 8.3 %conditional.2 = (f32[128,8,128]{2,0,1:T(8,128)S(1)}) conditional(s32[]{:T(128)} %convert_element_type.56, f32[128,8,128]{2,0,1:T(8,128)S(1)} %broadcast_in_dim.116, (s32[128]{0:T(128)S(1)}, s32[128]{0:T(128)S(1)}, bf16[2048,1024]{1,0:T(8,128)(2,1)}, bf16[128,8,128]{2,1,0:T(8,128)(2,1)S(1)}, f32[128]{0:T(128)S(1)}, ...), branch_computations={%region_9.10_spmd, %region_10.11_spmd} | conditional | flops 1091436544 | bytes 10225160 | solution.py:80
  194.2 7.0 %fusion.8 = f32[128,8,128]{2,0,1:T(8,128)S(1)} fusion(f32[128,8,128]{2,0,1:T(8,128)S(1)} %get-tuple-element.88, f32[128]{0:T(128)S(1)} %get-tuple-element.116, pred[128,2048]{1,0:T(8,128)(4,1)} %fusion.13, bf16[128,8,128]{2,1,0:T(8,128)(2,1)S(1)} %get-tuple-element.214, bf16[2048,1024]{1,0:T(8,128)(2,1)} %get-tuple-element.117, ...), kind=kOutput, calls=%fused_computation.15 | convolution fusion | flops 1090650112 | bytes 9961984 | tf_op jit(solution)/shard_map/while/body/eval_jaxpr/cond/branch_1_fun/hqk,khe->qhe/dot_general | solution.py:48
  201.6 2.1 fusion.79
  203.7 2.0 fusion.88
  205.7 22.3 %conditional.3 = (f32[2048,8,128]{2,0,1:T(8,128)}, f32[2048,8,128]{2,0,1:T(8,128)S(1)}, f32[128,8,128]{2,0,1:T(8,128)S(1)}) conditional(s32[]{:T(128)} %convert_element_type.56, f32[128,8,128]{2,0,1:T(8,128)S(1)} %broadcast_in_dim.116, (s32[128]{0:T(128)S(1)}, s32[128]{0:T(128)S(1)}, bf16[128,1024]{1,0:T(8,128)(2,1)S(1)}, ...), branch_computations={%region_15.16_spmd, %region_16.17_spmd} | conditional | flops 2729312256 | bytes 103549008 | solution.py:80
  208.4 5.5 %select_convert_fusion.2 = bf16[8,128,2048]{2,1,0:T(8,128)(2,1)S(1)} fusion(f32[8,128,2048]{2,1,0:T(8,128)S(1)} %fusion.21, f32[128]{0:T(128)S(1)} %get-tuple-element.124, pred[128,2048]{1,0:T(8,128)(4,1)S(1)} %fusion.37, bf16[2048,1024]{1,0:T(8,128)(2,1)S(1)} %copy-done.9, bf16[128,1024]{1,0:T(8,128)(2,1)S(1)} %get-tuple-element.120), kind=kOutput, calls=%fused_computation.22 | convolution fusion | flops 564133888 | bytes 17302016 | tf_op jit(solution)/shard_map/while/body/eval_jaxpr/cond/branch_1_fun/qhe,khe->hqk/dot_general | solution.py:59
  213.8 2.0 copy-done.5
  217.3 3.7 convolution_bitcast_fusion
  221.0 7.0 %convolution_bitcast_fusion.1 = f32[2048,8,128]{2,0,1:T(8,128)} fusion(bf16[8,128,2048]{2,1,0:T(8,128)(2,1)} %copy-done.5, bf16[128,8,128]{2,1,0:T(8,128)(2,1)S(1)} %get-tuple-element.223), kind=kOutput, calls=%fused_computation.25 | convolution fusion | flops 536870912 | bytes 12845056 | tf_op jit(solution)/shard_map/while/body/eval_jaxpr/cond/branch_1_fun/hqk,qhe->khe/dot_general | solution.py:70
  228.0 4.4 copy_bitcast_fusion.1
  232.7 7.8 %copy_bitcast_fusion = f32[2048,1024]{1,0:T(8,128)} fusion(f32[2048,8,128]{2,0,1:T(8,128)} %get-tuple-element.148), kind=kLoop, calls=%fused_computation.52 | loop fusion | bytes 16777216 | tf_op jit(solution)/shard_map/reshape | solution.py:200
  240.5 2.0 copy_bitcast_fusion.2
  242.5 89.3 %reduce-scatter.3.cloned.1.call-done = f32[128,1024]{1,0:T(8,128)} async-done(((f32[2048,1024]{1,0:T(8,128)}), f32[128,1024]{1,0:T(8,128)}) %reduce-scatter.3.cloned.1.call-update) | async-done | bytes 524304 | tf_op jit(solution)/shard_map/reduce_scatter | solution.py:202
  331.8 105.4 %reduce-scatter.5.cloned.1.call-done = f32[128,1024]{1,0:T(8,128)} async-done(((f32[2048,1024]{1,0:T(8,128)}), f32[128,1024]{1,0:T(8,128)}) %reduce-scatter.5.cloned.1.call-update) | async-done | bytes 524304 | tf_op jit(solution)/shard_map/reduce_scatter | solution.py:199
  437.2 8.4 %fusion.90 = (f32[128]{0:T(128)S(1)}, f32[128]{0:T(128)S(1)}, f32[128,1024]{1,0:T(8,128)}) fusion(f32[128]{0:T(128)S(1)} %add_rsqrt_fusion.1, f32[128,1024]{1,0:T(8,128)S(1)} %copy-done.2, f32[128]{0:T(128)S(1)} %broadcast_multiply_fusion.6, bf16[1024,4096]{1,0:T(8,128)(2,1)} %param.17, f32[128,1024]{1,0:T(8,128)} %reduce-scatter.5.cloned.1.call-done, ...), kind=kOutput, calls=%fused_computation.132 | convolution fusion | flops 1080688384 | bytes 13633536 | tf_op jit(solution)/shard_map/rk,dk->rd/dot_general | solution.py:213
  445.6 2.7 scatter_custom_fusion.1
  448.3 2.9 reshape.284
  451.2 9.1 %all-to-all-start.2 = ((f32[128,2,1024]{2,1,0:T(2,128)}), f32[128,2,1024]{2,1,0:T(2,128)}, u32[]{:S(2)}, u32[]{:S(2)}) async-start(f32[128,2,1024]{2,1,0:T(2,128)} %reshape.284), calls=%async_computation.4 | async-start | bytes 2097152 | tf_op jit(solution)/shard_map/all_to_all | solution.py:216
  460.5 2.2 fusion.51
  462.6 16.3 %all-to-all-done.2 = f32[128,2,1024]{2,1,0:T(2,128)} async-done(((f32[128,2,1024]{2,1,0:T(2,128)}), f32[128,2,1024]{2,1,0:T(2,128)}, u32[]{:S(2)}, u32[]{:S(2)}) %all-to-all-start.2) | async-done | bytes 1048608 | tf_op jit(solution)/shard_map/all_to_all | solution.py:216
  478.9 1.9 reshape.285
  480.9 6.6 %scatter_custom_fusion.2 = f32[2048,1024]{1,0:T(8,128)} fusion(s32[256]{0:T(256)S(1)} %reshape.290, f32[]{:T(128)} %constant.69.clone.1, f32[256,1024]{1,0:T(8,128)S(1)} %reshape.285, pred[256]{0:T(512)(128)(4,1)S(1)} %gt.23), kind=kCustom, calls=%fused_computation.55 | custom fusion | flops 524288 | bytes 9438720 | tf_op jit(solution)/shard_map/scatter-add | solution.py:226
  487.5 7.4 %broadcast_multiply_fusion = f32[2048,1024]{1,0:T(8,128)} fusion(f32[2048,1024]{1,0:T(8,128)} %scatter_custom_fusion.2, f32[2048]{0:T(1024)S(1)} %copy-done.1), kind=kLoop, calls=%fused_computation.54 | loop fusion | flops 2097152 | bytes 16785408 | tf_op jit(solution)/shard_map/mul | solution.py:228
  (71 shorter events, 22.9 us)
Async XLA Ops:
  7.2 194.4 %copy-start = (bf16[1024,1024]{1,0:T(8,128)(2,1)S(1)}, bf16[1024,1024]{1,0:T(8,128)(2,1)}, u32[]{:S(2)}) copy-start(bf16[1024,1024]{1,0:T(8,128)(2,1)} %param.18) | copy-start | bytes 6291460
  43.6 24.3 %all-to-all-start.1 = ((f32[128,2,1024]{2,1,0:T(2,128)}), f32[128,2,1024]{2,1,0:T(2,128)}, u32[]{:S(2)}, u32[]{:S(2)}) async-start(f32[128,2,1024]{2,1,0:T(2,128)} %multiply_select_fusion), calls=%async_computation.1 | async-start | bytes 2097152 | tf_op jit(solution)/shard_map/all_to_all | solution.py:120
  49.2 85.7 %all-gather.5.cloned.1.call-start = ((), (), s32[]{:S(2)}) async-start(), calls=%async_computation.6 | async-start | bytes 4456448 | tf_op jit(solution)/shard_map/all_gather | solution.py:144
  73.8 9.6 %copy-start.8 = (s32[1,3]{1,0:T(1,128)S(1)}, s32[1,3]{1,0:T(1,128)}, u32[]{:S(2)}) copy-start(s32[1,3]{1,0:T(1,128)} %param.16) | copy-start | bytes 40
  80.2 1.0 copy-start.6
  82.0 110.8 %all-gather.3.cloned.1.call-start = ((), (), s32[]{:S(2)}) async-start(), calls=%async_computation.5 | async-start | bytes 4456448 | tf_op jit(solution)/shard_map/all_gather | solution.py:143
  82.8 249.0 %reduce-scatter.3.cloned.1.call-start = ((), (), s32[]{:S(2)}) async-start(), calls=%async_computation.7 | async-start | bytes 8912896 | tf_op jit(solution)/shard_map/reduce_scatter | solution.py:202
  201.3 4.4 copy-start.4
  206.2 2.2 copy-start.9
  213.8 2.0 copy-start.5
  228.0 4.4 copy-start.3
  232.4 204.8 %reduce-scatter.5.cloned.1.call-start = ((), (), s32[]{:S(2)}) async-start(), calls=%async_computation.8 | async-start | bytes 8912896 | tf_op jit(solution)/shard_map/reduce_scatter | solution.py:199
  240.5 196.7 %copy-start.2 = (f32[128,1024]{1,0:T(8,128)S(1)}, f32[128,1024]{1,0:T(8,128)}, u32[]{:S(2)}) copy-start(f32[128,1024]{1,0:T(8,128)} %gather_fusion.2) | copy-start | bytes 1572868
  437.2 8.4 %copy-start.7 = (bf16[128,1024]{1,0:T(8,128)(2,1)S(1)}, bf16[128,1024]{1,0:T(8,128)(2,1)}, u32[]{:S(2)}) copy-start(bf16[128,1024]{1,0:T(8,128)(2,1)} %param.19) | copy-start | bytes 786436
  451.2 27.7 %all-to-all-start.2 = ((f32[128,2,1024]{2,1,0:T(2,128)}), f32[128,2,1024]{2,1,0:T(2,128)}, u32[]{:S(2)}, u32[]{:S(2)}) async-start(f32[128,2,1024]{2,1,0:T(2,128)} %reshape.284), calls=%async_computation.4 | async-start | bytes 2097152 | tf_op jit(solution)/shard_map/all_to_all | solution.py:216
  480.8 6.7 %copy-start.1 = (f32[2048]{0:T(1024)S(1)}, f32[2048]{0:T(1024)}, u32[]{:S(2)}) copy-start(f32[2048]{0:T(1024)} %param.13) | copy-start | bytes 24580
Sparse Core Ops, SparseCore 0:
  82.1 52.7 all-gather.4
  137.9 54.9 all-gather.2
  232.5 99.2 reduce-scatter.2
  336.0 101.1 reduce-scatter.4
where the time goes:
time: 502 us; the launch traced here: 501 us
  waiting for transfers between devices  337 us (67%)
  matrix products  44.9 us (9%)
  local copies, waits for them, and re-layouts  38.4 us (8%)
  other arithmetic  29.3 us (6%)
  blocking collectives  20.8 us (4%)
  between operations  15.3 us (3%)
  starting transfers between devices  15.1 us (3%)
    reduce_scatter x1, waiting for transfers between devices, per_device(): lax.psum_scatter(grad_key_all.reshape(key_total, model_width), 'cp', scat...  105 us
    reduce_scatter x1, waiting for transfers between devices, per_device(): lax.psum_scatter(grad_value_all.reshape(key_total, model_width), 'cp', sc...  89.3 us
    all_gather x1, waiting for transfers between devices, per_device(): lax.all_gather(key_rows, 'cp', axis=0, tiled=True)  57.9 us
    all_gather x1, waiting for transfers between devices, per_device(): lax.all_gather(value_rows, 'cp', axis=0, tiled=True)  49.2 us
    all_to_all x1, blocking collectives, per_device(): lax.all_to_all(requests.reshape(devices, capacity), ('dp', 'cp'), split_a...  20.8 us
    all_to_all x1, waiting for transfers between devices, per_device(): lax.all_to_all(fetched.reshape(devices, capacity, model_width), ('dp', 'c...  18.6 us
    all_to_all x1, waiting for transfers between devices, per_device(): lax.all_to_all(outgoing.reshape(devices, capacity, model_width), ('dp', '...  16.3 us
  transfers between devices with their start and end apart: 6, of which 6 were waited for; matrix products, arithmetic and copies ran while one was open for 3% of the time, Pallas kernels for 0%

commit v1 on v0

--- a/solution.py
+++ b/solution.py
@@ -139,8 +139,11 @@
     query_first, query_length = doc_bounds(lengths, cycle_pos)
     lowest = jnp.min(query_first)
     highest = cycle_pos[row_count - 1]
+    _arrange_loops = lambda x_in, dim_i: jnp.concatenate(
+        lax.all_to_all(jnp.stack(lax.psum(1, "cp") * [x_in], axis=0), "cp", 0, 0), dim_i
+    )
     key_all, value_all = (
-        lax.all_gather(key_rows, "cp", axis=0, tiled=True),
+        _arrange_loops(key_rows, 0),
         lax.all_gather(value_rows, "cp", axis=0, tiled=True),
     )
     key_total = key_all.shape[0]

time: 502 us -> 493 us (0.982); the launches traced: 501 us -> 484 us
  waiting for transfers between devices: 337 us -> 301 us
  local copies, waits for them, and re-layouts: 38.4 us -> 49.3 us
  starting transfers between devices: 15.1 us -> 20.4 us
    all_to_all x0 -> x1, waiting for transfers between devices: none -> 62.4 us  [per_device(): lax.all_to_all(jnp.stack(lax.psum(1, 'cp') * [x_in], axis=0), 'cp', 0, 0)]
    all_gather x1 -> x0, waiting for transfers between devices: 57.9 us -> none  [per_device(): lax.all_gather(key_rows, 'cp', axis=0, tiled=True)]
    all_gather x1, waiting for transfers between devices: 49.2 us -> 8.54 us  [per_device(): lax.all_gather(value_rows, 'cp', axis=0, tiled=True)]
    cond x4 -> x6, local copies, waits for them, and re-layouts: 2.84 us -> 11.4 us
    all_to_all x0 -> x1, starting transfers between devices: none -> 5.43 us  [per_device(): lax.all_to_all(jnp.stack(lax.psum(1, 'cp') * [x_in], axis=0), 'cp', 0, 0)]
where the time goes in v1:
time: 493 us; the launch traced here: 484 us
  waiting for transfers between devices  301 us (61%)
  local copies, waits for them, and re-layouts  49.3 us (10%)
  matrix products  47 us (10%)
  other arithmetic  29.3 us (6%)
  blocking collectives  20.8 us (4%)
  starting transfers between devices  20.4 us (4%)
  between operations  15.5 us (3%)
    reduce_scatter x1, waiting for transfers between devices, per_device(): lax.psum_scatter(grad_key_all.reshape(key_total, model_width), 'cp', scat...  106 us
    reduce_scatter x1, waiting for transfers between devices, per_device(): lax.psum_scatter(grad_value_all.reshape(key_total, model_width), 'cp', sc...  89.9 us
    all_to_all x1, waiting for transfers between devices, per_device(): lax.all_to_all(jnp.stack(lax.psum(1, 'cp') * [x_in], axis=0), 'cp', 0, 0)  62.4 us
    all_to_all x1, blocking collectives, per_device(): lax.all_to_all(requests.reshape(devices, capacity), ('dp', 'cp'), split_a...  20.8 us
    all_to_all x1, waiting for transfers between devices, per_device(): lax.all_to_all(fetched.reshape(devices, capacity, model_width), ('dp', 'c...  18.6 us
    all_to_all x1, waiting for transfers between devices, per_device(): lax.all_to_all(outgoing.reshape(devices, capacity, model_width), ('dp', '...  16.3 us
    cond x6, local copies, waits for them, and re-layouts  11.4 us
  transfers between devices with their start and end apart: 6, of which 6 were waited for; matrix products, arithmetic and copies ran while one was open for 3% of the time, Pallas kernels for 0%

profile of v1, /device:TPU:1, one launch (start us, length us, event | category | flops | bytes accessed | tf_op | source)
XLA Modules:
  0.0 484.3 jit_solution(3061758293601893756)
XLA Ops:
  11.5 20.8 %all_to_all.24 = s32[128,1,2]{2,1,0:T(1,128)S(1)} all-to-all(s32[128,1,2]{2,1,0:T(1,128)S(1)} %bitcast.120), channel_id=1, replica_groups=mesh['dp'=8,'cp'=16] {'dp','cp'}, dimensions={0} | all-to-all | bytes 2048 | tf_op jit(solution)/shard_map/all_to_all | solution.py:112
  35.3 5.1 %gather_fusion = bf16[256,1024]{1,0:T(8,128)(2,1)} fusion(bf16[2048,1024]{1,0:T(8,128)(2,1)} %param.12, s32[1024]{0:T(1024)S(1)} %pad_clamp_fusion.1), kind=kCustom, calls=%fused_computation | custom fusion | bytes 1049600 | tf_op jit(solution)/shard_map/gather | solution.py:118
  43.6 5.6 %all-to-all-start.1 = ((f32[128,2,1024]{2,1,0:T(2,128)}), f32[128,2,1024]{2,1,0:T(2,128)}, u32[]{:S(2)}, u32[]{:S(2)}) async-start(f32[128,2,1024]{2,1,0:T(2,128)} %multiply_select_fusion), calls=%async_computation.1 | async-start | bytes 2097152 | tf_op jit(solution)/shard_map/all_to_all | solution.py:120
  49.2 18.6 %all-to-all-done.1 = f32[128,2,1024]{2,1,0:T(2,128)} async-done(((f32[128,2,1024]{2,1,0:T(2,128)}), f32[128,2,1024]{2,1,0:T(2,128)}, u32[]{:S(2)}, u32[]{:S(2)}) %all-to-all-start.1) | async-done | bytes 1048608 | tf_op jit(solution)/shard_map/all_to_all | solution.py:120
  73.8 6.3 %multiply_convert_fusion = (bf16[128,4096]{1,0:T(8,128)(2,1)S(1)}, f32[128,4096]{1,0:T(8,128)}) fusion(bf16[1024,4096]{1,0:T(8,128)(2,1)} %param.17, f32[128,1024]{1,0:T(8,128)} %gather_fusion.2, f32[128]{0:T(128)S(1)} %add_rsqrt_fusion.1, f32[128]{0:T(128)S(1)} %broadcast_multiply_fusion.6), kind=kOutput, calls=%fused_computation.57 | convolution fusion | flops 1076756480 | bytes 12059648 | tf_op jit(solution)/shard_map/dot_general | solution.py:129
  81.9 2.5 stack.2
  84.5 5.4 %all-to-all-start.2 = ((bf16[16,128,1024]{2,1,0:T(8,128)(2,1)}), bf16[16,128,1024]{2,1,0:T(8,128)(2,1)}, u32[]{:S(2)}, u32[]{:S(2)}) async-start(bf16[16,128,1024]{2,1,0:T(8,128)(2,1)} %stack.2), calls=%async_computation.2 | async-start | bytes 8388608 | tf_op jit(solution)/shard_map/all_to_all | solution.py:143
  92.8 62.4 %all-to-all-done.2 = bf16[16,128,1024]{2,1,0:T(8,128)(2,1)} async-done(((bf16[16,128,1024]{2,1,0:T(8,128)(2,1)}), bf16[16,128,1024]{2,1,0:T(8,128)(2,1)}, u32[]{:S(2)}, u32[]{:S(2)}) %all-to-all-start.2) | async-done | bytes 4194336 | tf_op jit(solution)/shard_map/all_to_all | solution.py:143
  155.2 8.5 %all-gather.2.cloned.1.call-done = bf16[2048,1024]{1,0:T(8,128)(2,1)} async-done(((bf16[128,1024]{1,0:T(8,128)(2,1)}), bf16[2048,1024]{1,0:T(8,128)(2,1)}) %all-gather.2.cloned.1.call-update) | async-done | bytes 4194320 | tf_op jit(solution)/shard_map/all_gather | solution.py:147
  163.8 15.7 %conditional.2 = (f32[128,8,128]{2,0,1:T(8,128)S(1)}) conditional(s32[]{:T(128)} %convert_element_type.56, f32[128,8,128]{2,0,1:T(8,128)S(1)} %broadcast_in_dim.116, (s32[128]{0:T(128)S(1)}, s32[128]{0:T(128)S(1)}, bf16[16,128,1024]{2,1,0:T(8,128)(2,1)}, bf16[128,8,128]{2,1,0:T(8,128)(2,1)S(1)}, f32[128]{0:T(128)S(1)}, ...), branch_computations={%region_9.10_spmd, %region_10.11_spmd} | conditional | flops 1091436544 | bytes 18613768 | solution.py:80
  165.5 5.3 %copy.95 = bf16[256,8,8,128]{3,2,1,0:T(8,128)(2,1)} copy(bf16[256,8,8,128]{3,1,2,0:T(8,128)(2,1)} %bitcast.18) | data formatting | bytes 8388608 | tf_op jit(solution)/shard_map/while/body/eval_jaxpr/cond
  170.8 8.8 %fusion.7 = f32[128,8,128]{2,0,1:T(8,128)S(1)} fusion(f32[128,8,128]{2,0,1:T(8,128)S(1)} %get-tuple-element.88, bf16[2048,8,128]{2,1,0:T(8,128)(2,1)} %bitcast.117, f32[128]{0:T(128)S(1)} %get-tuple-element.116, pred[128,2048]{1,0:T(8,128)(4,1)} %fusion.12, bf16[128,8,128]{2,1,0:T(8,128)(2,1)S(1)} %get-tuple-element.214, ...), kind=kOutput, calls=%fused_computation.14 | convolution fusion | flops 1090650112 | bytes 9961984 | tf_op jit(solution)/shard_map/while/body/eval_jaxpr/cond/branch_1_fun/hqk,khe->qhe/dot_general | solution.py:48
  179.9 2.0 fusion.76
  181.9 2.0 fusion.85
  183.9 26.1 %conditional.3 = (f32[2048,8,128]{2,0,1:T(8,128)}, f32[2048,8,128]{2,0,1:T(8,128)S(1)}, f32[128,8,128]{2,0,1:T(8,128)S(1)}) conditional(s32[]{:T(128)} %convert_element_type.56, f32[128,8,128]{2,0,1:T(8,128)S(1)} %broadcast_in_dim.116, (s32[128]{0:T(128)S(1)}, s32[128]{0:T(128)S(1)}, bf16[128,1024]{1,0:T(8,128)(2,1)S(1)}, ...), branch_computations={%region_15.16_spmd, %region_16.17_spmd} | conditional | flops 2729312256 | bytes 111937616 | solution.py:80
  184.0 3.3 copy.98
  190.0 5.5 %select_convert_fusion.2 = bf16[8,128,2048]{2,1,0:T(8,128)(2,1)S(1)} fusion(f32[8,128,2048]{2,1,0:T(8,128)S(1)} %fusion.26, f32[128]{0:T(128)S(1)} %get-tuple-element.124, pred[128,2048]{1,0:T(8,128)(4,1)S(1)} %fusion.34, bf16[2048,1024]{1,0:T(8,128)(2,1)S(1)} %copy-done.8, bf16[128,1024]{1,0:T(8,128)(2,1)S(1)} %get-tuple-element.120), kind=kOutput, calls=%fused_computation.21 | convolution fusion | flops 564133888 | bytes 17302016 | tf_op jit(solution)/shard_map/while/body/eval_jaxpr/cond/branch_1_fun/qhe,khe->hqk/dot_general | solution.py:59
  195.5 2.0 copy-done.4
  199.3 3.7 convolution_bitcast_fusion
  203.0 7.0 %convolution_bitcast_fusion.1 = f32[2048,8,128]{2,0,1:T(8,128)} fusion(bf16[8,128,2048]{2,1,0:T(8,128)(2,1)} %copy-done.4, bf16[128,8,128]{2,1,0:T(8,128)(2,1)S(1)} %get-tuple-element.223), kind=kOutput, calls=%fused_computation.24 | convolution fusion | flops 536870912 | bytes 12845056 | tf_op jit(solution)/shard_map/while/body/eval_jaxpr/cond/branch_1_fun/hqk,qhe->khe/dot_general | solution.py:70
  210.0 4.4 copy_bitcast_fusion.1
  214.7 7.8 %copy_bitcast_fusion = f32[2048,1024]{1,0:T(8,128)} fusion(f32[2048,8,128]{2,0,1:T(8,128)} %get-tuple-element.148), kind=kLoop, calls=%fused_computation.49 | loop fusion | bytes 16777216 | tf_op jit(solution)/shard_map/reshape | solution.py:203
  224.5 89.9 %reduce-scatter.3.cloned.1.call-done = f32[128,1024]{1,0:T(8,128)} async-done(((f32[2048,1024]{1,0:T(8,128)}), f32[128,1024]{1,0:T(8,128)}) %reduce-scatter.3.cloned.1.call-update) | async-done | bytes 524304 | tf_op jit(solution)/shard_map/reduce_scatter | solution.py:205
  314.4 105.5 %reduce-scatter.5.cloned.1.call-done = f32[128,1024]{1,0:T(8,128)} async-done(((f32[2048,1024]{1,0:T(8,128)}), f32[128,1024]{1,0:T(8,128)}) %reduce-scatter.5.cloned.1.call-update) | async-done | bytes 524304 | tf_op jit(solution)/shard_map/reduce_scatter | solution.py:202
  419.9 8.4 %fusion.87 = (f32[128]{0:T(128)S(1)}, f32[128]{0:T(128)S(1)}, f32[128,1024]{1,0:T(8,128)}) fusion(f32[128]{0:T(128)S(1)} %add_rsqrt_fusion.1, f32[128,1024]{1,0:T(8,128)S(1)} %copy-done.2, f32[128]{0:T(128)S(1)} %broadcast_multiply_fusion.6, bf16[1024,4096]{1,0:T(8,128)(2,1)} %param.17, f32[128,1024]{1,0:T(8,128)} %reduce-scatter.5.cloned.1.call-done, ...), kind=kOutput, calls=%fused_computation.129 | convolution fusion | flops 1080688384 | bytes 13633536 | tf_op jit(solution)/shard_map/rk,dk->rd/dot_general | solution.py:216
  428.3 2.7 scatter_custom_fusion.1
  431.0 2.9 reshape.280
  433.9 9.1 %all-to-all-start.3 = ((f32[128,2,1024]{2,1,0:T(2,128)}), f32[128,2,1024]{2,1,0:T(2,128)}, u32[]{:S(2)}, u32[]{:S(2)}) async-start(f32[128,2,1024]{2,1,0:T(2,128)} %reshape.280), calls=%async_computation.5 | async-start | bytes 2097152 | tf_op jit(solution)/shard_map/all_to_all | solution.py:219
  443.1 2.2 fusion.48
  445.3 16.3 %all-to-all-done.3 = f32[128,2,1024]{2,1,0:T(2,128)} async-done(((f32[128,2,1024]{2,1,0:T(2,128)}), f32[128,2,1024]{2,1,0:T(2,128)}, u32[]{:S(2)}, u32[]{:S(2)}) %all-to-all-start.3) | async-done | bytes 1048608 | tf_op jit(solution)/shard_map/all_to_all | solution.py:219
  463.5 6.6 %scatter_custom_fusion.2 = f32[2048,1024]{1,0:T(8,128)} fusion(s32[256]{0:T(256)S(1)} %reshape.286, f32[]{:T(128)} %constant.69.clone.1, f32[256,1024]{1,0:T(8,128)S(1)} %reshape.281, pred[256]{0:T(512)(128)(4,1)S(1)} %gt.23), kind=kCustom, calls=%fused_computation.52 | custom fusion | flops 524288 | bytes 9438720 | tf_op jit(solution)/shard_map/scatter-add | solution.py:229
  470.2 7.4 %broadcast_multiply_fusion = f32[2048,1024]{1,0:T(8,128)} fusion(f32[2048,1024]{1,0:T(8,128)} %scatter_custom_fusion.2, f32[2048]{0:T(1024)S(1)} %copy-done.1), kind=kLoop, calls=%fused_computation.51 | loop fusion | flops 2097152 | bytes 16785408 | tf_op jit(solution)/shard_map/mul | solution.py:231
  (71 shorter events, 30.2 us)
Async XLA Ops:
  7.2 172.7 %copy-start = (bf16[1024,1024]{1,0:T(8,128)(2,1)S(1)}, bf16[1024,1024]{1,0:T(8,128)(2,1)}, u32[]{:S(2)}) copy-start(bf16[1024,1024]{1,0:T(8,128)(2,1)} %param.18) | copy-start | bytes 6291460
  43.6 24.3 %all-to-all-start.1 = ((f32[128,2,1024]{2,1,0:T(2,128)}), f32[128,2,1024]{2,1,0:T(2,128)}, u32[]{:S(2)}, u32[]{:S(2)}) async-start(f32[128,2,1024]{2,1,0:T(2,128)} %multiply_select_fusion), calls=%async_computation.1 | async-start | bytes 2097152 | tf_op jit(solution)/shard_map/all_to_all | solution.py:120
  49.2 114.6 %all-gather.2.cloned.1.call-start = ((), (), s32[]{:S(2)}) async-start(), calls=%async_computation.6 | async-start | bytes 4456448 | tf_op jit(solution)/shard_map/all_gather | solution.py:147
  80.1 1.0 copy-start.5
  80.1 10.4 %copy-start.7 = (s32[1,3]{1,0:T(1,128)S(1)}, s32[1,3]{1,0:T(1,128)}, u32[]{:S(2)}) copy-start(s32[1,3]{1,0:T(1,128)} %param.16) | copy-start | bytes 40
  84.5 70.8 %all-to-all-start.2 = ((bf16[16,128,1024]{2,1,0:T(8,128)(2,1)}), bf16[16,128,1024]{2,1,0:T(8,128)(2,1)}, u32[]{:S(2)}, u32[]{:S(2)}) async-start(bf16[16,128,1024]{2,1,0:T(8,128)(2,1)} %stack.2), calls=%async_computation.2 | async-start | bytes 8388608 | tf_op jit(solution)/shard_map/all_to_all | solution.py:143
  89.9 224.4 %reduce-scatter.3.cloned.1.call-start = ((), (), s32[]{:S(2)}) async-start(), calls=%async_computation.7 | async-start | bytes 8912896 | tf_op jit(solution)/shard_map/reduce_scatter | solution.py:205
  187.8 2.2 copy-start.8
  195.4 2.0 copy-start.4
  210.0 4.7 copy-start.3
  214.4 205.4 %reduce-scatter.5.cloned.1.call-start = ((), (), s32[]{:S(2)}) async-start(), calls=%async_computation.8 | async-start | bytes 8912896 | tf_op jit(solution)/shard_map/reduce_scatter | solution.py:202
  222.5 197.4 %copy-start.2 = (f32[128,1024]{1,0:T(8,128)S(1)}, f32[128,1024]{1,0:T(8,128)}, u32[]{:S(2)}) copy-start(f32[128,1024]{1,0:T(8,128)} %gather_fusion.2) | copy-start | bytes 1572868
  419.9 8.4 %copy-start.6 = (bf16[128,1024]{1,0:T(8,128)(2,1)S(1)}, bf16[128,1024]{1,0:T(8,128)(2,1)}, u32[]{:S(2)}) copy-start(bf16[128,1024]{1,0:T(8,128)(2,1)} %param.19) | copy-start | bytes 786436
  433.9 36.3 %copy-start.1 = (f32[2048]{0:T(1024)S(1)}, f32[2048]{0:T(1024)}, u32[]{:S(2)}) copy-start(f32[2048]{0:T(1024)} %param.13) | copy-start | bytes 24580
  433.9 27.7 %all-to-all-start.3 = ((f32[128,2,1024]{2,1,0:T(2,128)}), f32[128,2,1024]{2,1,0:T(2,128)}, u32[]{:S(2)}, u32[]{:S(2)}) async-start(f32[128,2,1024]{2,1,0:T(2,128)} %reshape.280), calls=%async_computation.5 | async-start | bytes 2097152 | tf_op jit(solution)/shard_map/all_to_all | solution.py:219
Sparse Core Ops, SparseCore 0:
  82.0 81.6 all-gather.1
  214.6 99.7 reduce-scatter.2
  318.7 101.1 reduce-scatter.4
